TPU v7x, 256 devices: a whole 4x4x8 slice. The times are simulated.
256 devices in a mesh: tm: 16 (over x, y_lo, core), batch: 16 (over z, y_hi).
Axes of the slice: x: 4, y: 4 (y_hi: 2, y_lo: 2; y = y_hi * 2 + y_lo), z: 8, core: 2. Of those that a mesh axis runs over, the one named last changes fastest.
Arguments:
- signal: bfloat16 [16, 2048, 4096], P('batch', 'tm'), may hold values from -7.5 to 7.5
- gate_input: bfloat16 [16, 2048, 4096], P('batch', 'tm'), may hold values from -6 to 6
- bc_forward: bfloat16 [16, 2048, 128], P('batch', 'tm'), may hold values from -6 to 6
- bc_backward: bfloat16 [16, 2048, 128], P('batch', 'tm'), may hold values from -6 to 6
- step_raw: bfloat16 [16, 2048, 128], P('batch', 'tm'), may hold values from -12 to 2
- decay_rate: float32 [2, 64], replicated, may hold values from 0.3 to 1
- conv_weight: float32 [2, 4, 4224], replicated, may hold values from -3 to 3
- conv_bias: float32 [2, 4224], replicated, may hold values from -1.5 to 1.5
- skip_gain: float32 [2, 64], replicated, may hold values from 0.5 to 1.5
- norm_gain: float32 [4096], replicated, may hold values from 0.1 to 1.9
Outputs:
- mixed: bfloat16 [16, 2048, 4096], P(None, 'batch', 'tm')
All inputs are finite; a program needn't handle non-finite values.
Results may differ from a plain program's by a relative error of at most 0.0075.
Values may be sent and summed in bfloat16 or wider, within the bound.
No kernel may reach another device: no remote copies, remote signals or barrier semaphores. Data moves between devices by JAX's collectives and lax.ppermute only.
A program may use at most 256 MiB of HBM per device.

v0:
```python
import jax
import jax.numpy as jnp
from jax import lax
from jax.sharding import PartitionSpec as P

INNER = 4096
HEADDIM = 64
STATE = 64
GROUP = 128
HEADS = 64
EPSILON = 1e-05


def from_behind(array, axis, by):
    devices = lax.axis_size(axis)
    pairs = [(i, i + by) for i in range(devices) if 0 <= i + by < devices]
    return lax.ppermute(array, axis, pairs)


def entering(value, axis, join, neutral):
    count, mine = (lax.axis_size(axis), lax.axis_index(axis))
    pieces = jax.tree.map(lambda part: lax.all_gather(part, axis), value)
    running = jax.tree.map(
        lambda part, zero: jnp.full_like(part, 0) + jnp.asarray(zero, part.dtype), value, neutral
    )

    def lap(position, running):
        longer = join(running, jax.tree.map(lambda part: part[position], pieces))
        return jax.tree.map(lambda new, old: jnp.where(position < mine, new, old), longer, running)

    return lax.fori_loop(0, count - 1, lap, running)


def carried_in(array, axis, join, neutral):
    count = lax.axis_size(axis)
    place = lax.axis_index(axis)
    ahead = count - 1 - place
    gathered = jax.tree.map(
        lambda a, kind: lax.all_gather(a.astype(kind), axis), array, (jnp.bfloat16, jnp.bfloat16)
    )
    state = jax.tree.map(lambda a, e: jnp.zeros_like(a) + jnp.asarray(e, a.dtype), array, neutral)

    def one(lap, state):
        source = count - 1 - lap
        return join(
            state,
            jax.tree.map(
                lambda a, own: lax.dynamic_index_in_dim(a, source, 0, False).astype(own.dtype),
                gathered,
                array,
            ),
        )

    return lax.fori_loop(0, ahead, one, state)


def conv_silu(sequence, history, weights, offsets):
    length = sequence.shape[0]
    padded = jnp.concatenate([history, sequence], 0).astype(jnp.float32)
    combined_waveform = jnp.broadcast_to(offsets[None, :], (length, sequence.shape[1]))
    for offset in range(weights.shape[0]):
        combined_waveform = (
            combined_waveform + weights[offset][None, :] * padded[offset : offset + length]
        )
    return jax.nn.silu(combined_waveform).astype(jnp.bfloat16)


def block_parts(x_part, b_part, step_size, rate_head):
    log_decay = -step_size * rate_head[None, None, :]
    cum_log = jnp.cumsum(log_decay, axis=1)
    weight_end = jnp.exp(cum_log[:, -1:, :] - cum_log) * step_size
    b_scaled = (b_part.astype(jnp.float32)[:, :, None, :] * weight_end[..., None]).astype(
        jnp.bfloat16
    )
    states = jnp.einsum("mqhn,mqhp->mhnp", b_scaled, x_part, preferred_element_type=jnp.float32)
    return (cum_log, states, jnp.exp(cum_log[:, -1, :]))


def prepare(x_conv, bc_conv, step_raw, rate_head):
    block_count = x_conv.shape[0] // GROUP
    x_part = x_conv.reshape(block_count, GROUP, -1, HEADDIM)
    b_part = bc_conv[:, :STATE].reshape(block_count, GROUP, STATE)
    c_part = bc_conv[:, STATE:].reshape(block_count, GROUP, STATE)
    step_size = jax.nn.softplus(step_raw.astype(jnp.float32)).reshape(block_count, GROUP, -1)
    cum_log, states, decays = block_parts(x_part, b_part, step_size, rate_head)
    return (x_part, b_part, c_part, step_size, cum_log, states, decays)


def summarize(states, decays):

    def absorb(state_in, pieces):
        return (pieces[1][:, None, None] * state_in + pieces[0], None)

    final_state, _ = lax.scan(absorb, jnp.zeros(states.shape[1:], jnp.float32), (states, decays))
    return (jnp.prod(decays, axis=0), final_state)


def carried_term(c_block, state_in):
    state_high = state_in.astype(jnp.bfloat16)
    state_low = (state_in - state_high.astype(jnp.float32)).astype(jnp.bfloat16)
    upper = jnp.einsum("in,hnp->ihp", c_block, state_high, preferred_element_type=jnp.float32)
    lower = jnp.einsum("in,hnp->ihp", c_block, state_low, preferred_element_type=jnp.float32)
    return upper + lower


def block_outputs(parts, start, skip_head):
    block_len = parts[0].shape[1]
    causal_mask = jnp.arange(block_len)[:, None] >= jnp.arange(block_len)[None, :]

    def advance(state_in, pieces):
        x_block, b_block, c_block, step_block, cum_block, state_block, decay_block = pieces
        scores = jnp.dot(c_block, b_block.T, preferred_element_type=jnp.float32)
        differ = cum_block.T[:, :, None] - cum_block.T[:, None, :]
        masked = jnp.where(causal_mask[None], jnp.exp(jnp.minimum(differ, 0.0)), 0.0)
        mixing = (masked * scores[None] * step_block.T[:, None, :]).astype(jnp.bfloat16)
        local_out = jnp.einsum("hij,jhp->ihp", mixing, x_block, preferred_element_type=jnp.float32)
        carried = carried_term(c_block, state_in)
        result = (
            local_out
            + jnp.exp(cum_block)[:, :, None] * carried
            + skip_head[None, :, None] * x_block.astype(jnp.float32)
        )
        new_state = decay_block[:, None, None] * state_in + state_block
        return (new_state, result.astype(jnp.bfloat16))

    _, outputs = lax.scan(advance, start, parts)
    return outputs.reshape(outputs.shape[0] * outputs.shape[1], -1)


def combine(earlier, later):
    return (earlier[0] * later[0], earlier[1] * later[0][:, None, None] + later[1])


def gated_rows(forward_out, backward_out, gate_rows):
    return (forward_out.astype(jnp.float32) + backward_out.astype(jnp.float32)) * jax.nn.silu(
        gate_rows.astype(jnp.float32)
    )


def shards(
    signal,
    gate_input,
    bc_forward,
    bc_backward,
    step_raw,
    decay_rate,
    conv_weight,
    conv_bias,
    skip_gain,
    norm_gain,
):
    rim_rows = conv_weight.shape[1] - 1
    signal_dev = signal[0]
    bcf_dev = bc_forward[0]
    bcb_dev = bc_backward[0]
    step_dev = step_raw[0]
    left_rim = from_behind(
        jnp.concatenate([signal_dev[-rim_rows:], bcf_dev[-rim_rows:]], 1), "tm", 1
    )
    right_rim = from_behind(
        jnp.concatenate([signal_dev[:rim_rows], bcb_dev[:rim_rows]], 1), "tm", -1
    )
    fwd_parts = prepare(
        conv_silu(signal_dev, left_rim[:, :INNER], conv_weight[0, :, :INNER], conv_bias[0, :INNER]),
        conv_silu(bcf_dev, left_rim[:, INNER:], conv_weight[0, :, INNER:], conv_bias[0, INNER:]),
        step_dev[:, :HEADS],
        decay_rate[0],
    )
    back_history = right_rim[::-1]
    bwd_parts = prepare(
        conv_silu(
            signal_dev[::-1],
            back_history[:, :INNER],
            conv_weight[1, :, :INNER],
            conv_bias[1, :INNER],
        ),
        conv_silu(
            bcb_dev[::-1], back_history[:, INNER:], conv_weight[1, :, INNER:], conv_bias[1, INNER:]
        ),
        step_dev[::-1, HEADS:],
        decay_rate[1],
    )
    fwd_decay, fwd_state = summarize(fwd_parts[5], fwd_parts[6])
    bwd_decay, bwd_state = summarize(bwd_parts[5], bwd_parts[6])
    empty_decay = jnp.ones((HEADS,), jnp.float32)
    empty_state = jnp.zeros((HEADS, STATE, HEADDIM), jnp.float32)
    fwd_in = entering((fwd_decay, fwd_state), "tm", combine, (empty_decay, empty_state))
    bwd_in = carried_in((bwd_decay, bwd_state), "tm", combine, (empty_decay, empty_state))
    forward_out = block_outputs(fwd_parts, fwd_in[1], skip_gain[0])
    backward_out = block_outputs(bwd_parts, bwd_in[1], skip_gain[1])[::-1]
    gated = gated_rows(forward_out, backward_out, gate_input[0])
    inv_rms = lax.rsqrt(jnp.mean(gated * gated, axis=-1, keepdims=True) + EPSILON)
    normed = (gated * inv_rms * norm_gain[None, :]).astype(jnp.bfloat16)
    return lax.all_to_all(
        lax.all_to_all(normed[None], "tm", split_axis=2, concat_axis=1, tiled=True),
        "batch",
        split_axis=1,
        concat_axis=0,
        tiled=True,
    )


def solution(mesh):
    in_specs = (
        P("batch", "tm", None),
        P("batch", "tm", None),
        P("batch", "tm", None),
        P("batch", "tm", None),
        P("batch", "tm", None),
        P(),
        P(),
        P(),
        P(),
        P(),
    )
    out_specs = P(None, "batch", "tm")
    return jax.shard_map(shards, mesh=mesh, in_specs=in_specs, out_specs=out_specs, check_vma=False)
```

profile of v0, /device:TPU:8, one launch (start us, length us, event | category | flops | bytes accessed | tf_op | source)
XLA Modules:
  0.0 470.2 jit_solution(14375612540284527570)
XLA Ops:
  10.9 3.6 collective-permute-start.1
  34.6 2.4 add_convert_fusion
  42.8 17.5 %all-gather.2 = bf16[16,1,64]{2,1,0:T(2,128)(2,1)S(1)} all-gather(bf16[1,1,64]{2,1,0:T(2,128)(2,1)S(1)} %copy-done.21), channel_id=4, replica_groups=mesh['tm'=16,'batch'=16] {'tm'}, dimensions={0}, use_global_device_ids=true | all-gather | bytes 2176 | tf_op jit(solution)/shard_map/all_gather | solution.py:39
  61.1 18.7 %all-gather = f32[16,1,64]{2,1,0:T(1,128)S(1)} all-gather(f32[1,1,64]{2,1,0:T(1,128)S(1)} %get-tuple-element.350), channel_id=2, replica_groups=mesh['tm'=16,'batch'=16] {'tm'}, dimensions={0}, use_global_device_ids=true | all-gather | bytes 4352 | tf_op jit(solution)/shard_map/all_gather | solution.py:22
  80.2 54.8 %all-gather.9.cloned.1.call-done = bf16[1024,64,64]{2,1,0:T(8,128)(2,1)} async-done(((bf16[64,64,64]{2,1,0:T(8,128)(2,1)}), bf16[1024,64,64]{2,1,0:T(8,128)(2,1)}) %all-gather.9.cloned.1.call-update) | async-done | bytes 8388624 | tf_op jit(solution)/shard_map/all_gather | solution.py:39
  135.3 23.3 %while.18 = (s32[]{:T(128)}, f32[64,64,64]{2,1,0:T(8,128)S(1)}, s32[]{:T(128)}, bf16[16,64]{1,0:T(8,128)(2,1)S(1)}, bf16[16,64,64,64]{3,2,1,0:T(8,128)(2,1)}, /*index=5*/s32[]{:T(128)}, s32[]{:T(128)}, s32[]{:T(128)}, s32[]{:T(128)}) while((s32[]{:T(128)}, f32[64,64,64]{2,1,0:T(8,128)S(1)}, s32[]{:T(128)}, bf16[16,64]{1,0:T(8,128)(2,1)S(1)}, ...), condition=%wide.region_5.6_spmd, body=%wide.region_4.5_spmd.sunk | while | flops 786502 | bytes 2622235 | solution.py:54
  164.0 2.5 fusion.16
  167.9 12.6 %rev.16 = bf16[128,4096]{1,0:T(8,128)(2,1)S(1)} reverse(bf16[128,4096]{1,0:T(8,128)(2,1)} %copy.108), dimensions={0} | reverse | bytes 2097152 | tf_op jit(solution)/shard_map/rev | solution.py:190
  180.5 130.4 %all-gather.7.cloned.1.call-done = f32[1024,64,64]{2,1,0:T(8,128)} async-done(((f32[64,64,64]{2,1,0:T(8,128)}), f32[1024,64,64]{2,1,0:T(8,128)}) %all-gather.7.cloned.1.call-update) | async-done | bytes 16777232 | tf_op jit(solution)/shard_map/all_gather | solution.py:22
  310.9 31.9 %while.19 = (s32[]{:T(128)}, f32[64,64,64]{2,1,0:T(8,128)S(1)}, s32[]{:T(128)}, f32[16,64]{1,0:T(8,128)S(1)}, f32[16,64,64,64]{3,2,1,0:T(8,128)}, /*index=5*/s32[]{:T(128)}, s32[]{:T(128)}) while((s32[]{:T(128)}, f32[64,64,64]{2,1,0:T(8,128)S(1)}, s32[]{:T(128)}, f32[16,64]{1,0:T(8,128)S(1)}, f32[16,64,64,64]{3,2,1,0:T(8,128)}, ...), condition=%wide.region_2.3_spmd.clone, body=%wide.region_1.2_spmd.clone.sunk | while | flops 1048580 | bytes 3146609 | solution.py:31
  313.0 2.1 fusion.86
  315.1 2.1 fusion.86
  317.2 2.1 fusion.86
  319.4 2.1 fusion.86
  321.5 2.1 fusion.86
  323.6 2.1 fusion.86
  325.8 2.1 fusion.86
  327.9 2.1 fusion.86
  330.0 2.1 fusion.86
  332.1 2.1 fusion.86
  334.3 2.1 fusion.86
  336.4 2.1 fusion.86
  338.5 2.1 fusion.86
  340.6 2.1 fusion.86
  350.6 2.5 fusion.18
  356.6 2.1 multiply_reduce_fusion
  359.0 2.8 copy.110
  362.4 22.4 %reduce = bf16[4096,128]{1,0:T(8,128)(2,1)S(1)} reduce(bf16[4096,1,128]{2,1,0:T(2,128)(2,1)S(1)} %bitcast.171, bf16[]{:T(256)} %broadcast.103), dimensions={1}, to_apply=%bitcast.145.reduce_sub_computation | reduce | bytes 2097154
  385.1 20.0 %all_to_all.30 = bf16[16,2,16384]{2,1,0:T(2,128)(2,1)S(1)} all-to-all(bf16[16,2,16384]{2,1,0:T(2,128)(2,1)S(1)} %reshape.251), channel_id=1, replica_groups=mesh['tm'=16,'batch'=16] {'tm'}, dimensions={0} | all-to-all | bytes 2097152 | tf_op jit(solution)/shard_map/all_to_all | solution.py:195
  407.6 3.2 copy.119
  410.8 10.6 %reduce.1 = bf16[2048,256]{1,0:T(8,128)(2,1)S(1)} reduce(bf16[2048,1,256]{2,1,0:T(2,128)(2,1)S(1)} %bitcast.172, bf16[]{:T(256)} %broadcast.103), dimensions={1}, to_apply=%bitcast.160.reduce_sub_computation | reduce | bytes 2097154
  421.7 39.5 %all_to_all.31 = bf16[16,2,16384]{2,1,0:T(2,128)(2,1)S(1)} all-to-all(bf16[16,2,16384]{2,1,0:T(2,128)(2,1)S(1)} %reshape.253), channel_id=1, replica_groups=mesh['tm'=16,'batch'=16] {'batch'}, dimensions={0} | all-to-all | bytes 2097152 | tf_op jit(solution)/shard_map/all_to_all | solution.py:194
  (176 shorter events, 80.3 us)
Async XLA Ops:
  6.5 19.8 %copy-start.1 = (bf16[1,128,4096]{2,1,0:T(8,128)(2,1)S(1)}, bf16[1,128,4096]{2,1,0:T(8,128)(2,1)}, u32[]{:S(2)}) copy-start(bf16[1,128,4096]{2,1,0:T(8,128)(2,1)} %param.14) | copy-start | bytes 3145732
  6.5 128.5 %all-gather.9.cloned.1.call-start = ((), (), s32[]{:S(2)}) async-start(), calls=%async_computation.3 | async-start | bytes 17825792 | tf_op jit(solution)/shard_map/all_gather | solution.py:39
  8.2 20.9 %collective-permute-start = (bf16[3,4224]{1,0:T(4,128)(2,1)S(1)}, bf16[3,4224]{1,0:T(4,128)(2,1)S(1)}, u32[]{:S(2)}, u32[]{:S(2)}) collective-permute-start(bf16[3,4224]{1,0:T(4,128)(2,1)S(1)} %pad_maximum_fusion), channel_id=1, source_target_pairs={{0,16},{16,32},{32,48},{48,64},{64,80},{80,96},{96,112},{112,128},... | collective-permute-start | bytes 76040 | tf_op jit(solution)/shard_map/ppermute | solution.py:17
  10.9 17.4 %collective-permute-start.1 = (bf16[3,4224]{1,0:T(4,128)(2,1)S(1)}, bf16[3,4224]{1,0:T(4,128)(2,1)S(1)}, u32[]{:S(2)}, u32[]{:S(2)}) collective-permute-start(bf16[3,4224]{1,0:T(4,128)(2,1)S(1)} %pad_maximum_fusion.1), channel_id=1, source_target_pairs={{16,0},{32,16},{48,32},{64,48},{80,64},{96,80},{112,96},{128,112},... | collective-permute-start | bytes 76040 | tf_op jit(solution)/shard_map/ppermute | solution.py:17
  29.2 1.9 copy-start.15
  32.4 0.8 copy-start.9
  32.4 0.8 copy-start.10
  33.2 3.9 copy-start.6
  33.4 3.9 copy-start.8
  34.5 2.9 copy-start.16
  37.0 0.8 copy-start.11
  37.0 0.8 copy-start.12
  37.0 0.8 copy-start.13
  37.1 0.8 copy-start.14
  37.1 273.8 %all-gather.7.cloned.1.call-start = ((), (), s32[]{:S(2)}) async-start(), calls=%async_computation.2 | async-start | bytes 35651584 | tf_op jit(solution)/shard_map/all_gather | solution.py:22
  39.8 2.0 copy-start.2
  39.9 2.9 copy-start.21
  41.9 38.0 %copy-start.20 = (f32[2,64]{1,0:T(2,128)S(1)}, f32[2,64]{1,0:T(2,128)}, u32[]{:S(2)}) copy-start(f32[2,64]{1,0:T(2,128)} %param.22) | copy-start | bytes 1540
  162.8 1.2 copy-start.7
  162.8 1.2 copy-start.18
  166.5 144.3 %copy-start = (f32[64,64,64]{2,1,0:T(8,128)S(1)}, f32[64,64,64]{2,1,0:T(8,128)}, u32[]{:S(2)}) copy-start(f32[64,64,64]{2,1,0:T(8,128)} %custom-call) | copy-start | bytes 3145732
  346.2 1.8 copy-start.4
  348.0 1.1 copy-start.17
  348.7 1.2 copy-start.3
  348.7 1.9 copy-start.5
  356.6 2.1 copy-start.19
Sparse Core Ops, SparseCore 0:
  37.1 97.8 all-gather.8
  136.9 173.9 all-gather.6
where the time goes:
time: 474 us; the launch traced here: 470 us
  waiting for transfers between devices  185 us (39%)
  other arithmetic  101 us (21%)
  blocking collectives  95.7 us (20%)
  local copies, waits for them, and re-layouts  54.4 us (11%)
  between operations  14 us (3%)
  matrix products  12.7 us (3%)
  starting transfers between devices  5.61 us (1%)
    all_gather x1, waiting for transfers between devices, entering(): pieces = jax.tree.map(lambda part: lax.all_gather(part, axis), value)  130 us
    all_gather x1, waiting for transfers between devices, carried_in(): lax.all_gather(a.astype(kind), axis)  54.8 us
    all_to_all x1, blocking collectives, shards(): lax.all_to_all(lax.all_to_all(normed[None], 'tm', split_axis=2, concat_ax...  39.5 us
    unnamed x3, other arithmetic  33 us
    select_n x15, other arithmetic, lap(): jnp.where(position < mine, new, old)  31.2 us
    add x13, other arithmetic, combine(): earlier[1] * later[0][:, None, None] + later[1]  22.5 us
    all_to_all x1, blocking collectives, shards(): lax.all_to_all(normed[None], 'tm', split_axis=2, concat_axis=1, tiled=True)  20 us
    all_gather x1, blocking collectives, entering(): pieces = jax.tree.map(lambda part: lax.all_gather(part, axis), value)  18.7 us
  transfers between devices with their start and end apart: 4, of which 2 were waited for; matrix products, arithmetic and copies ran while one was open for 14% of the time, Pallas kernels for 0%

commit v1 on v0

--- a/solution.py
+++ b/solution.py
@@ -192,7 +192,12 @@
     inv_rms = lax.rsqrt(jnp.mean(gated * gated, axis=-1, keepdims=True) + EPSILON)
     normed = (gated * inv_rms * norm_gain[None, :]).astype(jnp.bfloat16)
     return lax.all_to_all(
-        lax.all_to_all(normed[None], "tm", split_axis=2, concat_axis=1, tiled=True),
+        jnp.concatenate(
+            lax.all_to_all(
+                jnp.stack(jnp.split(normed[None], lax.axis_size("tm"), axis=2)), "tm", 0, 0
+            ),
+            axis=1,
+        ),
         "batch",
         split_axis=1,
         concat_axis=0,

time: 474 us -> 454 us (0.958)
  other arithmetic: 101 us -> 78.9 us
    unnamed x3 -> x2, other arithmetic: 33 us -> 10.6 us
    reshape x0 -> x1, local copies, waits for them, and re-layouts: none -> 11.6 us  [shards(): jnp.concatenate(lax.all_to_all(jnp.stack(jnp.split(normed[None], lax.axis...]
  transfers between devices with their start and end apart: 4 -> 4, of which waited for: 2 -> 2; matrix products, arithmetic and copies ran while one was open for 14% -> 15% of each run, Pallas kernels for 0% -> 0%
where the time goes in v1:
time: 454 us; the launch traced here: 451 us
  waiting for transfers between devices  185 us (41%)
  blocking collectives  95.7 us (21%)
  other arithmetic  78.9 us (17%)
  local copies, waits for them, and re-layouts  57.5 us (13%)
  between operations  14.1 us (3%)
  matrix products  12.7 us (3%)
  starting transfers between devices  5.61 us (1%)
    all_gather x1, waiting for transfers between devices, entering(): pieces = jax.tree.map(lambda part: lax.all_gather(part, axis), value)  130 us
    all_gather x1, waiting for transfers between devices, carried_in(): lax.all_gather(a.astype(kind), axis)  54.8 us
    all_to_all x1, blocking collectives, shards(): lax.all_to_all(jnp.concatenate(lax.all_to_all(jnp.stack(jnp.split(normed[...  39.5 us
    select_n x15, other arithmetic, lap(): jnp.where(position < mine, new, old)  31.2 us
    add x13, other arithmetic, combine(): earlier[1] * later[0][:, None, None] + later[1]  22.5 us
    all_to_all x1, blocking collectives, shards(): lax.all_to_all(jnp.stack(jnp.split(normed[None], lax.axis_size('tm'), axi...  20 us
    all_gather x1, blocking collectives, entering(): pieces = jax.tree.map(lambda part: lax.all_gather(part, axis), value)  18.7 us
    all_gather x1, blocking collectives, carried_in(): lax.all_gather(a.astype(kind), axis)  17.5 us
  transfers between devices with their start and end apart: 4, of which 2 were waited for; matrix products, arithmetic and copies ran while one was open for 15% of the time, Pallas kernels for 0%

profile of v1, /device:TPU:8, one launch (start us, length us, event | category | flops | bytes accessed | tf_op | source)
XLA Modules:
  0.0 450.9 jit_solution(13164768544550479103)
XLA Ops:
  10.9 3.6 collective-permute-start.1
  34.6 2.4 add_convert_fusion
  42.8 17.5 %all-gather.2 = bf16[16,1,64]{2,1,0:T(2,128)(2,1)S(1)} all-gather(bf16[1,1,64]{2,1,0:T(2,128)(2,1)S(1)} %copy-done.21), channel_id=4, replica_groups=mesh['tm'=16,'batch'=16] {'tm'}, dimensions={0}, use_global_device_ids=true | all-gather | bytes 2176 | tf_op jit(solution)/shard_map/all_gather | solution.py:39
  61.1 18.7 %all-gather = f32[16,1,64]{2,1,0:T(1,128)S(1)} all-gather(f32[1,1,64]{2,1,0:T(1,128)S(1)} %get-tuple-element.350), channel_id=2, replica_groups=mesh['tm'=16,'batch'=16] {'tm'}, dimensions={0}, use_global_device_ids=true | all-gather | bytes 4352 | tf_op jit(solution)/shard_map/all_gather | solution.py:22
  80.2 54.8 %all-gather.9.cloned.1.call-done = bf16[1024,64,64]{2,1,0:T(8,128)(2,1)} async-done(((bf16[64,64,64]{2,1,0:T(8,128)(2,1)}), bf16[1024,64,64]{2,1,0:T(8,128)(2,1)}) %all-gather.9.cloned.1.call-update) | async-done | bytes 8388624 | tf_op jit(solution)/shard_map/all_gather | solution.py:39
  135.3 23.3 %while.18 = (s32[]{:T(128)}, f32[64,64,64]{2,1,0:T(8,128)S(1)}, s32[]{:T(128)}, bf16[16,64]{1,0:T(8,128)(2,1)S(1)}, bf16[16,64,64,64]{3,2,1,0:T(8,128)(2,1)}, /*index=5*/s32[]{:T(128)}, s32[]{:T(128)}, s32[]{:T(128)}, s32[]{:T(128)}) while((s32[]{:T(128)}, f32[64,64,64]{2,1,0:T(8,128)S(1)}, s32[]{:T(128)}, bf16[16,64]{1,0:T(8,128)(2,1)S(1)}, ...), condition=%wide.region_5.6_spmd, body=%wide.region_4.5_spmd.sunk | while | flops 786502 | bytes 2622235 | solution.py:54
  149.3 2.0 convert_add_fusion.2
  164.1 2.5 fusion.16
  167.9 12.6 %rev.16 = bf16[128,4096]{1,0:T(8,128)(2,1)S(1)} reverse(bf16[128,4096]{1,0:T(8,128)(2,1)} %copy.143), dimensions={0} | reverse | bytes 2097152 | tf_op jit(solution)/shard_map/rev | solution.py:190
  180.5 130.4 %all-gather.7.cloned.1.call-done = f32[1024,64,64]{2,1,0:T(8,128)} async-done(((f32[64,64,64]{2,1,0:T(8,128)}), f32[1024,64,64]{2,1,0:T(8,128)}) %all-gather.7.cloned.1.call-update) | async-done | bytes 16777232 | tf_op jit(solution)/shard_map/all_gather | solution.py:22
  310.9 31.9 %while.19 = (s32[]{:T(128)}, f32[64,64,64]{2,1,0:T(8,128)S(1)}, s32[]{:T(128)}, f32[16,64]{1,0:T(8,128)S(1)}, f32[16,64,64,64]{3,2,1,0:T(8,128)}, /*index=5*/s32[]{:T(128)}, s32[]{:T(128)}) while((s32[]{:T(128)}, f32[64,64,64]{2,1,0:T(8,128)S(1)}, s32[]{:T(128)}, f32[16,64]{1,0:T(8,128)S(1)}, f32[16,64,64,64]{3,2,1,0:T(8,128)}, ...), condition=%wide.region_2.3_spmd.clone, body=%wide.region_1.2_spmd.clone.sunk | while | flops 1048580 | bytes 3146609 | solution.py:31
  310.9 2.1 fusion.102
  313.0 2.1 fusion.102
  315.1 2.1 fusion.102
  317.3 2.1 fusion.102
  319.4 2.1 fusion.102
  321.5 2.1 fusion.102
  323.6 2.1 fusion.102
  325.8 2.1 fusion.102
  327.9 2.1 fusion.102
  330.0 2.1 fusion.102
  332.2 2.1 fusion.102
  334.3 2.1 fusion.102
  336.4 2.1 fusion.102
  338.5 2.1 fusion.102
  340.7 2.1 fusion.102
  350.6 2.5 fusion.18
  356.6 2.1 multiply_reduce_fusion
  359.3 20.0 %all_to_all.17 = bf16[16,1,128,256]{3,2,1,0:T(8,128)(2,1)S(1)} all-to-all(bf16[16,1,128,256]{3,2,1,0:T(8,128)(2,1)S(1)} %fusion.44), channel_id=1, replica_groups=mesh['tm'=16,'batch'=16] {'tm'}, dimensions={0} | all-to-all | bytes 2097152 | tf_op jit(solution)/shard_map/all_to_all | solution.py:196
  379.3 11.6 %copy.151 = bf16[1,2048,256]{2,0,1:T(2,128)(2,1)S(1)} copy(bf16[1,2048,256]{2,1,0:T(8,128)(2,1)S(1)} %bitcast.236) | data formatting | bytes 2097152 | tf_op jit(solution)/shard_map/reshape | solution.py:195
  391.5 10.6 %reduce = bf16[2048,256]{1,0:T(8,128)(2,1)S(1)} reduce(bf16[2048,1,256]{2,1,0:T(2,128)(2,1)S(1)} %bitcast.229, bf16[]{:T(256)} %broadcast.103), dimensions={1}, to_apply=%bitcast.219.reduce_sub_computation | reduce | bytes 2097154
  402.4 39.5 %all_to_all.18 = bf16[16,2,16384]{2,1,0:T(2,128)(2,1)S(1)} all-to-all(bf16[16,2,16384]{2,1,0:T(2,128)(2,1)S(1)} %reshape.255), channel_id=1, replica_groups=mesh['tm'=16,'batch'=16] {'batch'}, dimensions={0} | all-to-all | bytes 2097152 | tf_op jit(solution)/shard_map/all_to_all | solution.py:194
  (186 shorter events, 73.6 us)
Async XLA Ops:
  6.5 19.8 %copy-start.1 = (bf16[1,128,4096]{2,1,0:T(8,128)(2,1)S(1)}, bf16[1,128,4096]{2,1,0:T(8,128)(2,1)}, u32[]{:S(2)}) copy-start(bf16[1,128,4096]{2,1,0:T(8,128)(2,1)} %param.14) | copy-start | bytes 3145732
  6.5 128.5 %all-gather.9.cloned.1.call-start = ((), (), s32[]{:S(2)}) async-start(), calls=%async_computation.3 | async-start | bytes 17825792 | tf_op jit(solution)/shard_map/all_gather | solution.py:39
  8.2 20.9 %collective-permute-start = (bf16[3,4224]{1,0:T(4,128)(2,1)S(1)}, bf16[3,4224]{1,0:T(4,128)(2,1)S(1)}, u32[]{:S(2)}, u32[]{:S(2)}) collective-permute-start(bf16[3,4224]{1,0:T(4,128)(2,1)S(1)} %pad_maximum_fusion), channel_id=1, source_target_pairs={{0,16},{16,32},{32,48},{48,64},{64,80},{80,96},{96,112},{112,128},... | collective-permute-start | bytes 76040 | tf_op jit(solution)/shard_map/ppermute | solution.py:17
  10.9 17.4 %collective-permute-start.1 = (bf16[3,4224]{1,0:T(4,128)(2,1)S(1)}, bf16[3,4224]{1,0:T(4,128)(2,1)S(1)}, u32[]{:S(2)}, u32[]{:S(2)}) collective-permute-start(bf16[3,4224]{1,0:T(4,128)(2,1)S(1)} %pad_maximum_fusion.1), channel_id=1, source_target_pairs={{16,0},{32,16},{48,32},{64,48},{80,64},{96,80},{112,96},{128,112},... | collective-permute-start | bytes 76040 | tf_op jit(solution)/shard_map/ppermute | solution.py:17
  29.1 1.9 copy-start.15
  32.4 0.8 copy-start.9
  32.4 0.8 copy-start.10
  33.2 3.9 copy-start.6
  33.3 4.0 copy-start.8
  34.6 2.9 copy-start.16
  37.0 0.8 copy-start.11
  37.1 0.8 copy-start.12
  37.1 0.8 copy-start.13
  37.1 0.8 copy-start.14
  37.1 273.8 %all-gather.7.cloned.1.call-start = ((), (), s32[]{:S(2)}) async-start(), calls=%async_computation.2 | async-start | bytes 35651584 | tf_op jit(solution)/shard_map/all_gather | solution.py:22
  39.9 2.0 copy-start.2
  39.9 2.9 copy-start.21
  41.9 38.0 %copy-start.20 = (f32[2,64]{1,0:T(2,128)S(1)}, f32[2,64]{1,0:T(2,128)}, u32[]{:S(2)}) copy-start(f32[2,64]{1,0:T(2,128)} %param.22) | copy-start | bytes 1540
  162.8 1.2 copy-start.7
  162.8 1.2 copy-start.18
  166.5 144.3 %copy-start = (f32[64,64,64]{2,1,0:T(8,128)S(1)}, f32[64,64,64]{2,1,0:T(8,128)}, u32[]{:S(2)}) copy-start(f32[64,64,64]{2,1,0:T(8,128)} %custom-call) | copy-start | bytes 3145732
  346.3 1.8 copy-start.4
  348.0 1.1 copy-start.17
  348.7 1.2 copy-start.3
  348.7 1.9 copy-start.5
  356.6 2.1 copy-start.19
Sparse Core Ops, SparseCore 0:
  37.2 97.8 all-gather.8
  136.9 173.9 all-gather.6
